TPU v7x, 32 devices: a whole 2x2x4 slice. The times are simulated.
32 devices in a mesh: parts: 2 (over y), expert: 8 (over z, x), group: 1, tensor: 2 (over core).
Axes of the slice: x: 2, y: 2, z: 4, core: 2. Of those that a mesh axis runs over, the one named last changes fastest.
Arguments:
- hidden_in: bfloat16 [3, 64, 4096], P(None, ('parts', 'expert', 'group')), parts along dimension 1, may hold values from -6 to 6
- queries: bfloat16 [3, 64, 32, 128], P(None, ('parts', 'expert', 'group'), 'tensor'), parts along dimension 1, may hold values from -32 to 32
- new_keys: bfloat16 [3, 64, 4, 128], P(None, ('parts', 'expert', 'group'), 'tensor'), parts along dimension 1, may hold values from -4 to 4
- new_values: bfloat16 [3, 64, 4, 128], P(None, ('parts', 'expert', 'group'), 'tensor'), parts along dimension 1, may hold values from -8 to 8
- cache_keys: bfloat16 [64, 4, 128, 128], P(('parts', 'expert', 'group'), 'tensor'), parts along dimension 0, may hold values from -4 to 4
- cache_values: bfloat16 [64, 4, 128, 128], P(('parts', 'expert', 'group'), 'tensor'), parts along dimension 0, may hold values from -8 to 8
- route_ids: int32 [3, 64, 8], P(None, ('parts', 'expert', 'group')), parts along dimension 1, may hold values from 0 to 15, all different within a row; in each aligned block of 4 rows (0 to 3, 4 to 7, ..., all dimensions but the last counted through in order) at most 4 rows name the same one
- route_weights: float32 [3, 64, 8], P(None, ('parts', 'expert', 'group')), parts along dimension 1, may hold values from 0.1 to 1
- norm_gain: float32 [4096], replicated, may hold values from 0.25 to 1.75
- gate_weight: bfloat16 [16, 4096, 768], P('expert', 'group', 'tensor'), may hold values from -0.09375 to 0.09375
- up_weight: bfloat16 [16, 4096, 768], P('expert', 'group', 'tensor'), may hold values from -0.09375 to 0.09375
- down_weight: bfloat16 [16, 768, 4096], P('expert', None, ('group', 'tensor')), may hold values from -0.21875 to 0.21875
- ancestor_counts: int32 [64], P(('parts', 'expert', 'group')), parts along dimension 0, may hold values from 0 to 5, as said below
Outputs:
- layer_out: bfloat16 [3, 64, 4096], P(None, ('parts', 'expert', 'group')), parts along dimension 1
- resampled_keys: bfloat16 [64, 4, 131, 128], P(('parts', 'expert', 'group'), 'tensor'), parts along dimension 0
- resampled_values: bfloat16 [64, 4, 131, 128], P(('parts', 'expert', 'group'), 'tensor'), parts along dimension 0
There are 2 independent parts, one for each index of `parts`. A program takes and returns all parts, laid end to end along the dimension named above; an argument that names none is the same for every part. Nothing has to cross between parts.
Inputs may be any that keep to these rules, and one draw needn't show every extreme that they name: `route_ids`: each row names 8 different experts; in each aligned block of 4 rows (the rows of one device in one step) no expert is named by more than 4 rows. `ancestor_counts`: the counts sum to 32, and every particle i descends from a particle within 2 positions of i.
All inputs are finite; a program needn't handle non-finite values.
Results may differ from a plain program's by a relative error of at most 0.0075.
Values may be sent and summed in bfloat16 or wider, within the bound.
A program may use at most 64 MiB of HBM per device.

v0:
```python
import math

import jax
import jax.numpy as jnp
from jax import lax
from jax.sharding import PartitionSpec as P

REACH = 2


epsilon = 1e-06
highest = lax.Precision.HIGHEST


def padded(cells, sides, width):
    for axis, dim in sides:
        count = lax.axis_size(axis)
        ends = count - 1
        head = lax.slice_in_dim(cells, 0, width, axis=dim)
        tail = lax.slice_in_dim(cells, cells.shape[dim] - width, cells.shape[dim], axis=dim)
        cells = jnp.concatenate(
            [
                lax.ppermute(tail, axis, [(i, (i + 1) % count) for i in range(ends)]),
                cells,
                lax.ppermute(head, axis, [((i + 1) % count, i) for i in range(ends)]),
            ],
            axis=dim,
        )
    return cells


def shards(
    hidden_in,
    queries,
    new_keys,
    new_values,
    cache_keys,
    cache_values,
    route_ids,
    route_weights,
    norm_gain,
    gate_weight,
    up_weight,
    down_weight,
    ancestor_counts,
):
    step_count, token_count, query_heads, head_width = queries.shape
    key_heads = cache_keys.shape[1]
    cached = cache_keys.shape[2]
    group_size = query_heads // key_heads
    cache_pair = jnp.stack([cache_keys, cache_values])
    fresh_pair = jnp.transpose(jnp.stack([new_keys, new_values]), (0, 2, 3, 1, 4))
    both_kv = jnp.concatenate([cache_pair, fresh_pair], axis=3)
    length = both_kv.shape[3]
    grouped = queries.reshape(step_count, token_count, key_heads, group_size, head_width)
    scores = jnp.einsum(
        "sphgd,phld->sphgl", grouped, both_kv[0], preferred_element_type=jnp.float32
    ) / math.sqrt(head_width)
    allowed = lax.broadcasted_iota(
        jnp.int32, (step_count, length), 1
    ) <= cached + lax.broadcasted_iota(jnp.int32, (step_count, length), 0)
    scores = jnp.where(allowed[:, None, None, None, :], scores, -1e30)
    exponent = jnp.exp(scores - jnp.max(scores, axis=-1, keepdims=True))
    attn_weights = (exponent / jnp.sum(exponent, axis=-1, keepdims=True)).astype(jnp.bfloat16)
    attended = jnp.einsum(
        "sphgl,phld->sphgd", attn_weights, both_kv[1], preferred_element_type=jnp.float32
    )
    attended = attended.astype(jnp.bfloat16).reshape(
        step_count, token_count, query_heads * head_width
    )
    attended = lax.all_gather(attended, "tensor", axis=2, tiled=True)
    expert_count = lax.axis_size("expert")
    group_count = lax.axis_size("group")
    tensor_count = lax.axis_size("tensor")
    tensor_index = lax.axis_index("tensor")
    expert_local = gate_weight.shape[0]
    experts_all = expert_local * expert_count
    chosen_count = route_ids.shape[2]
    model_width = hidden_in.shape[2]
    column_width = down_weight.shape[2]
    capacity = min(token_count, max(2, 2 * token_count * chosen_count // experts_all))
    pair_count = token_count * chosen_count
    expert_iota = jnp.arange(experts_all, dtype=jnp.int32)
    slot_iota = jnp.arange(capacity, dtype=jnp.int32)
    token_owner = (
        (jnp.arange(pair_count) // chosen_count)[:, None] == jnp.arange(token_count)[None, :]
    ).astype(jnp.float32)
    halves = []
    for step_index in range(step_count):
        residual = hidden_in[step_index].astype(jnp.float32) + attended[step_index].astype(
            jnp.float32
        )
        normed = (
            residual
            * lax.rsqrt(jnp.mean(residual * residual, axis=-1, keepdims=True) + epsilon)
            * norm_gain
        ).astype(jnp.bfloat16)
        chosen = route_ids[step_index].reshape(pair_count)
        route_share = route_weights[step_index] / jnp.sum(
            route_weights[step_index], axis=-1, keepdims=True
        )
        expert_hits = (chosen[:, None] == expert_iota[None, :]).astype(jnp.int32)
        position = jnp.sum((jnp.cumsum(expert_hits, axis=0) - expert_hits) * expert_hits, axis=1)
        slotted = (
            expert_hits[:, :, None]
            * (position[:, None, None] == slot_iota[None, None, :]).astype(jnp.int32)
        ).astype(jnp.float32)
        dispatch = jnp.einsum("rec,rt->ect", slotted, token_owner, precision=highest)
        dispatch = dispatch.reshape(expert_count, expert_local, capacity, token_count).astype(
            jnp.bfloat16
        )
        combine = jnp.einsum(
            "rec,rt,r->tec",
            slotted,
            token_owner,
            route_share.reshape(pair_count),
            precision=highest,
        )
        combine = combine.reshape(token_count, expert_count, expert_local, capacity)
        feature_blocks = normed.reshape(token_count, group_count, model_width // group_count)
        outgoing = jnp.einsum(
            "aict,tgd->agicd", dispatch, feature_blocks, preferred_element_type=jnp.float32
        ).astype(jnp.bfloat16)
        flattened = outgoing.reshape(
            expert_count * group_count, expert_local, capacity, model_width // group_count
        )
        received = lax.all_to_all(
            flattened, ("expert", "group"), split_axis=0, concat_axis=0, tiled=True
        )
        gate_part = jnp.einsum(
            "seki,eif->sekf", received, gate_weight, preferred_element_type=jnp.float32
        ).astype(jnp.bfloat16)
        up_part = jnp.einsum(
            "seki,eif->sekf", received, up_weight, preferred_element_type=jnp.float32
        ).astype(jnp.bfloat16)
        gate_sum = lax.psum(gate_part, "group").astype(jnp.float32)
        up_sum = lax.psum(up_part, "group").astype(jnp.float32)
        hidden = (jax.nn.silu(gate_sum) * up_sum).astype(jnp.bfloat16)
        hidden = lax.all_gather(hidden, "tensor", axis=3, tiled=True)
        answered = jnp.einsum(
            "sekf,efo->seko", hidden, down_weight, preferred_element_type=jnp.float32
        ).astype(jnp.bfloat16)
        returned = lax.all_to_all(
            answered, ("expert", "group"), split_axis=0, concat_axis=0, tiled=True
        )
        returned = returned.reshape(
            expert_count, group_count, expert_local, capacity, column_width
        ).astype(jnp.float32)
        expert_mix = jnp.einsum("taic,agicd->tgd", combine, returned, precision=highest)
        own_columns = lax.dynamic_index_in_dim(
            residual.reshape(token_count, group_count, tensor_count, column_width),
            tensor_index,
            2,
            keepdims=False,
        )
        halves.append((own_columns + expert_mix).astype(jnp.bfloat16))
    stacked = jnp.stack(halves)
    layer_out = lax.all_gather(stacked, "tensor", axis=3, tiled=True).reshape(
        step_count, token_count, model_width
    )
    every_count = lax.all_gather(ancestor_counts, ("expert", "group"), axis=0, tiled=True)
    running = jnp.cumsum(every_count)
    first_index = lax.axis_index(("expert", "group")) * token_count
    own_index = first_index + jnp.arange(token_count, dtype=jnp.int32)
    ancestor = jnp.sum((running[None, :] <= own_index[:, None]).astype(jnp.int32), axis=1)
    widened = padded(both_kv, ((("expert", "group"), 1),), REACH)
    window_index = first_index - REACH + jnp.arange(token_count + 2 * REACH, dtype=jnp.int32)
    selector = (ancestor[:, None] == window_index[None, :]).astype(jnp.bfloat16)
    resampled = jnp.einsum(
        "tw,kwhld->kthld", selector, widened, preferred_element_type=jnp.float32
    ).astype(jnp.bfloat16)
    return (layer_out, resampled[0], resampled[1])


def solution(mesh):
    in_specs = (
        P(None, ("parts", "expert", "group"), None),
        P(None, ("parts", "expert", "group"), "tensor", None),
        P(None, ("parts", "expert", "group"), "tensor", None),
        P(None, ("parts", "expert", "group"), "tensor", None),
        P(("parts", "expert", "group"), "tensor", None, None),
        P(("parts", "expert", "group"), "tensor", None, None),
        P(None, ("parts", "expert", "group"), None),
        P(None, ("parts", "expert", "group"), None),
        P(),
        P("expert", "group", "tensor"),
        P("expert", "group", "tensor"),
        P("expert", None, ("group", "tensor")),
        P(("parts", "expert", "group")),
    )
    out_specs = (
        P(None, ("parts", "expert", "group"), None),
        P(("parts", "expert", "group"), "tensor", None, None),
        P(("parts", "expert", "group"), "tensor", None, None),
    )
    return jax.shard_map(shards, mesh=mesh, in_specs=in_specs, out_specs=out_specs, check_vma=False)
```

profile of v0, /device:TPU:0, one launch (start us, length us, event | category | flops | bytes accessed | tf_op | source)
XLA Modules:
  0.0 131.6 jit_solution(18216911250874261639)
XLA Ops:
  3.7 2.0 %all_gather.18 = bf16[3,4,4096]{2,1,0:T(4,128)(2,1)S(1)} all-gather(bf16[3,4,2048]{2,1,0:T(4,128)(2,1)S(1)} %reshape.678), channel_id=1, replica_groups=mesh['parts'=2,'expert'=8,'group'=1,'tensor'=2] {'tensor'}, dimensions={2}, use_global_device_ids=true | all-gather | bytes 147456 | tf_op jit(solution)/shard_map/all_gather | solution.py:71
  5.7 1.6 %multiply_reduce_fusion.2 = (f32[4]{0:T(128)S(1)}, f32[4]{0:T(128)S(1)}, f32[4]{0:T(128)S(1)}, f32[1,4,4096]{2,1,0:T(4,128)}, f32[1,4,4096]{2,1,0:T(4,128)}, /*index=5*/f32[1,4,4096]{2,1,0:T(4,128)}) fusion(bf16[3,4,4096]{2,1,0:T(4,128)(2,1)S(1)} %all_gather.18, bf16[3,4,4096]{2,1,0:T(4,128)(2,1)} %param.13), kind=kLoop, calls=%fused_computation.116 | loop fusion | flops 245748 | bytes 393264 | tf_op jit(solution)/shard_map/reduce_sum | solution.py:95
  8.9 1.1 fusion.19
  10.0 1.2 copy.114
  11.3 7.1 %all-to-all-start = ((bf16[8,2,4,4096]{3,2,1,0:T(4,128)(2,1)}), bf16[8,2,4,4096]{3,2,1,0:T(4,128)(2,1)S(1)}, u32[]{:S(2)}, u32[]{:S(2)}) async-start(bf16[8,2,4,4096]{3,2,1,0:T(4,128)(2,1)} %copy.114), calls=%async_computation | async-start | bytes 1048576 | tf_op jit(solution)/shard_map/all_to_all | solution.py:127
  18.4 3.9 %collective-permute-start = (bf16[2,2,2,131,128]{4,3,2,1,0:T(8,128)(2,1)S(1)}, bf16[2,2,2,131,128]{4,3,2,1,0:T(8,128)(2,1)S(1)}, u32[]{:S(2)}, u32[]{:S(2)}) collective-permute-start(bf16[2,2,2,131,128]{4,3,2,1,0:T(8,128)(2,1)S(1)} %get-tuple-element.21), channel_id=1, source_target_pairs={{0,2},{2,4},{4,6},{6,8},{8,10},{10,12},{12,14},{1,3},{3,5},{5,7},{... | collective-permute-start | bytes 804872 | tf_op jit(solution)/shard_map/ppermute | solution.py:23
  22.4 1.3 collective-permute-start.1
  28.3 1.2 copy.126
  29.7 1.2 copy.138
  31.2 1.2 dynamic-slice
  33.3 13.5 %all-reduce = s32[32]{0:T(128)S(1)} all-reduce(s32[32]{0:T(128)S(1)} %dynamic-update-slice), channel_id=1, replica_groups=mesh['parts'=2,'expert'=8,'group'=1,'tensor'=2] {'expert','group'}, use_global_device_ids=true, to_apply=%add | all-reduce | flops 32 | bytes 256
  47.9 4.3 %all-to-all-start.2 = ((bf16[8,2,4,4096]{3,2,1,0:T(4,128)(2,1)}), bf16[8,2,4,4096]{3,2,1,0:T(4,128)(2,1)}, u32[]{:S(2)}, u32[]{:S(2)}) async-start(bf16[8,2,4,4096]{3,2,1,0:T(4,128)(2,1)} %copy.126), calls=%async_computation.2 | async-start | bytes 1048576 | tf_op jit(solution)/shard_map/all_to_all | solution.py:127
  52.2 4.1 %fusion.60 = f32[8,2,4,384]{3,2,0,1:T(4,128)S(1)} fusion(bf16[2,4096,384]{2,1,0:T(8,128)(2,1)} %param.22, bf16[8,2,4,4096]{3,2,1,0:T(4,128)(2,1)S(1)} %all-to-all-done), kind=kOutput, calls=%fused_computation.52 | convolution fusion | flops 201375744 | bytes 6914048 | tf_op jit(solution)/shard_map/seki,eif->sekf/dot_general | solution.py:130
  56.4 1.2 fusion.123
  57.5 1.9 %all_gather.19 = bf16[8,2,4,768]{3,2,0,1:T(4,128)(2,1)S(1)} all-gather(bf16[8,2,4,384]{3,2,0,1:T(4,128)(2,1)S(1)} %fusion.123), channel_id=1, replica_groups=mesh['parts'=2,'expert'=8,'group'=1,'tensor'=2] {'tensor'}, dimensions={3}, use_global_device_ids=true | all-gather | bytes 147456 | tf_op jit(solution)/shard_map/all_gather | solution.py:139
  59.4 5.8 %all-to-all-done.2 = bf16[8,2,4,4096]{3,2,1,0:T(4,128)(2,1)} async-done(((bf16[8,2,4,4096]{3,2,1,0:T(4,128)(2,1)}), bf16[8,2,4,4096]{3,2,1,0:T(4,128)(2,1)}, u32[]{:S(2)}, u32[]{:S(2)}) %all-to-all-start.2) | async-done | bytes 524320 | tf_op jit(solution)/shard_map/all_to_all | solution.py:127
  65.2 3.8 %all-to-all-start.4 = ((bf16[8,2,4,4096]{3,2,1,0:T(4,128)(2,1)}), bf16[8,2,4,4096]{3,2,1,0:T(4,128)(2,1)S(1)}, u32[]{:S(2)}, u32[]{:S(2)}) async-start(bf16[8,2,4,4096]{3,2,1,0:T(4,128)(2,1)} %copy.138), calls=%async_computation.4 | async-start | bytes 1048576 | tf_op jit(solution)/shard_map/all_to_all | solution.py:127
  69.0 4.2 %fusion.69 = f32[8,2,4,384]{3,2,0,1:T(4,128)S(1)} fusion(bf16[2,4096,384]{2,1,0:T(8,128)(2,1)} %param.22, bf16[8,2,4,4096]{3,2,1,0:T(4,128)(2,1)} %all-to-all-done.2), kind=kOutput, calls=%fused_computation.55 | convolution fusion | flops 201375744 | bytes 6914048 | tf_op jit(solution)/shard_map/seki,eif->sekf/dot_general | solution.py:130
  73.3 1.1 fusion.37
  75.4 4.1 %fusion.117 = bf16[8,2,4,384]{3,2,0,1:T(4,128)(2,1)S(1)} fusion(bf16[2,4096,384]{2,1,0:T(8,128)(2,1)} %param.23, bf16[8,2,4,4096]{3,2,1,0:T(4,128)(2,1)} %all-to-all-done.2, f32[8,2,4,384]{3,2,0,1:T(4,128)S(1)} %fusion.69), kind=kOutput, calls=%fused_computation.72 | convolution fusion | flops 201523200 | bytes 6963200 | tf_op jit(solution)/shard_map/seki,eif->sekf/dot_general | solution.py:133
  79.5 2.1 %all_gather.20 = bf16[8,2,4,768]{3,2,0,1:T(4,128)(2,1)S(1)} all-gather(bf16[8,2,4,384]{3,2,0,1:T(4,128)(2,1)S(1)} %fusion.117), channel_id=1, replica_groups=mesh['parts'=2,'expert'=8,'group'=1,'tensor'=2] {'tensor'}, dimensions={3}, use_global_device_ids=true | all-gather | bytes 147456 | tf_op jit(solution)/shard_map/all_gather | solution.py:139
  81.6 1.1 fusion.34
  83.7 6.0 %all-to-all-start.1 = ((bf16[8,2,4,2048]{3,1,2,0:T(2,128)(2,1)}), bf16[8,2,4,2048]{3,1,2,0:T(2,128)(2,1)S(1)}, u32[]{:S(2)}, u32[]{:S(2)}) async-start(bf16[8,2,4,2048]{3,1,2,0:T(2,128)(2,1)} %copy.118), calls=%async_computation.1 | async-start | bytes 524288 | tf_op jit(solution)/shard_map/all_to_all | solution.py:143
  89.7 3.9 %fusion.78 = f32[8,2,4,384]{3,2,0,1:T(4,128)S(1)} fusion(bf16[2,4096,384]{2,1,0:T(8,128)(2,1)} %param.22, bf16[8,2,4,4096]{3,2,1,0:T(4,128)(2,1)S(1)} %all-to-all-done.4), kind=kOutput, calls=%fused_computation.58 | convolution fusion | flops 201375744 | bytes 6914048 | tf_op jit(solution)/shard_map/seki,eif->sekf/dot_general | solution.py:130
  93.7 5.3 %all-to-all-done.1 = bf16[8,2,4,2048]{3,1,2,0:T(2,128)(2,1)S(1)} async-done(((bf16[8,2,4,2048]{3,1,2,0:T(2,128)(2,1)}), bf16[8,2,4,2048]{3,1,2,0:T(2,128)(2,1)S(1)}, u32[]{:S(2)}, u32[]{:S(2)}) %all-to-all-start.1) | async-done | bytes 262176 | tf_op jit(solution)/shard_map/all_to_all | solution.py:143
  99.0 3.6 %all-to-all-start.3 = ((bf16[8,2,4,2048]{3,1,2,0:T(2,128)(2,1)}), bf16[8,2,4,2048]{3,1,2,0:T(2,128)(2,1)S(1)}, u32[]{:S(2)}, u32[]{:S(2)}) async-start(bf16[8,2,4,2048]{3,1,2,0:T(2,128)(2,1)} %copy.130), calls=%async_computation.3 | async-start | bytes 524288 | tf_op jit(solution)/shard_map/all_to_all | solution.py:143
  102.5 3.9 %fusion.111 = bf16[8,2,4,384]{3,2,0,1:T(4,128)(2,1)S(1)} fusion(bf16[2,4096,384]{2,1,0:T(8,128)(2,1)} %param.23, bf16[8,2,4,4096]{3,2,1,0:T(4,128)(2,1)S(1)} %all-to-all-done.4, f32[8,2,4,384]{3,2,0,1:T(4,128)S(1)} %fusion.78), kind=kOutput, calls=%fused_computation.70 | convolution fusion | flops 201523200 | bytes 6963200 | tf_op jit(solution)/shard_map/seki,eif->sekf/dot_general | solution.py:133
  106.5 2.0 %all_gather.21 = bf16[8,2,4,768]{3,2,0,1:T(4,128)(2,1)S(1)} all-gather(bf16[8,2,4,384]{3,2,0,1:T(4,128)(2,1)S(1)} %fusion.111), channel_id=1, replica_groups=mesh['parts'=2,'expert'=8,'group'=1,'tensor'=2] {'tensor'}, dimensions={3}, use_global_device_ids=true | all-gather | bytes 147456 | tf_op jit(solution)/shard_map/all_gather | solution.py:139
  108.5 3.9 %fusion.31 = bf16[8,2,4,2048]{3,0,1,2:T(8,128)(2,1)S(1)} fusion(bf16[2,768,2048]{2,1,0:T(8,128)(2,1)} %param.24, bf16[8,2,4,768]{3,2,0,1:T(4,128)(2,1)S(1)} %all_gather.21), kind=kOutput, calls=%fused_computation.28 | convolution fusion | flops 201457664 | bytes 6651904 | tf_op jit(solution)/shard_map/sekf,efo->seko/dot_general | solution.py:140
  113.4 6.0 %all-to-all-start.5 = ((bf16[8,2,4,2048]{3,1,2,0:T(2,128)(2,1)}), bf16[8,2,4,2048]{3,1,2,0:T(2,128)(2,1)S(1)}, u32[]{:S(2)}, u32[]{:S(2)}) async-start(bf16[8,2,4,2048]{3,1,2,0:T(2,128)(2,1)} %copy.142), calls=%async_computation.5 | async-start | bytes 524288 | tf_op jit(solution)/shard_map/all_to_all | solution.py:143
  122.2 6.4 %all-to-all-done.5 = bf16[8,2,4,2048]{3,1,2,0:T(2,128)(2,1)S(1)} async-done(((bf16[8,2,4,2048]{3,1,2,0:T(2,128)(2,1)}), bf16[8,2,4,2048]{3,1,2,0:T(2,128)(2,1)S(1)}, u32[]{:S(2)}, u32[]{:S(2)}) %all-to-all-start.5) | async-done | bytes 262176 | tf_op jit(solution)/shard_map/all_to_all | solution.py:143
  129.1 1.9 %all_gather.22 = bf16[3,4,1,4096]{3,1,2,0:T(4,128)(2,1)S(1)} all-gather(bf16[3,4,1,2048]{3,1,2,0:T(4,128)(2,1)S(1)} %pad_maximum_fusion.2), channel_id=1, replica_groups=mesh['parts'=2,'expert'=8,'group'=1,'tensor'=2] {'tensor'}, dimensions={3}, use_global_device_ids=true | all-gather | bytes 147456 | tf_op jit(solution)/shard_map/all_gather | solution.py:158
  (120 shorter events, 17.6 us)
Async XLA Ops:
  0.6 2.1 %copy-start = (bf16[3,4,16,128]{3,2,1,0:T(8,128)(2,1)S(1)}, bf16[3,4,16,128]{3,2,1,0:T(8,128)(2,1)}, u32[]{:S(2)}) copy-start(bf16[3,4,16,128]{3,2,1,0:T(8,128)(2,1)} %param.14) | copy-start | bytes 147460
  0.6 46.7 %copy-start.2 = (bf16[4,2,128,128]{3,2,1,0:T(8,128)(2,1)S(1)}, bf16[4,2,128,128]{3,2,1,0:T(8,128)(2,1)}, u32[]{:S(2)}) copy-start(bf16[4,2,128,128]{3,2,1,0:T(8,128)(2,1)} %param.17) | copy-start | bytes 786436
  0.7 46.7 %copy-start.1 = (bf16[4,2,128,128]{3,2,1,0:T(8,128)(2,1)S(1)}, bf16[4,2,128,128]{3,2,1,0:T(8,128)(2,1)}, u32[]{:S(2)}) copy-start(bf16[4,2,128,128]{3,2,1,0:T(8,128)(2,1)} %param.18) | copy-start | bytes 786436
  0.7 26.3 %copy-start.3 = (bf16[3,4,4096]{2,1,0:T(4,128)(2,1)S(1)}, bf16[3,4,4096]{2,1,0:T(4,128)(2,1)}, u32[]{:S(2)}) copy-start(bf16[3,4,4096]{2,1,0:T(4,128)(2,1)} %param.13) | copy-start | bytes 294916
  0.7 26.3 %copy-start.4 = (f32[4096]{0:T(1024)S(1)}, f32[4096]{0:T(1024)}, u32[]{:S(2)}) copy-start(f32[4096]{0:T(1024)} %param.21) | copy-start | bytes 49156
  0.7 23.6 %copy-start.8 = (f32[3,4,8]{2,1,0:T(4,128)S(1)}, f32[3,4,8]{2,1,0:T(4,128)}, u32[]{:S(2)}) copy-start(f32[3,4,8]{2,1,0:T(4,128)} %param.20) | copy-start | bytes 1156
  0.7 32.4 %copy-start.9 = (s32[4]{0:T(128)S(1)}, s32[4]{0:T(128)}, u32[]{:S(2)}) copy-start(s32[4]{0:T(128)} %param.25) | copy-start | bytes 52
  11.3 36.7 %all-to-all-start = ((bf16[8,2,4,4096]{3,2,1,0:T(4,128)(2,1)}), bf16[8,2,4,4096]{3,2,1,0:T(4,128)(2,1)S(1)}, u32[]{:S(2)}, u32[]{:S(2)}) async-start(bf16[8,2,4,4096]{3,2,1,0:T(4,128)(2,1)} %copy.114), calls=%async_computation | async-start | bytes 1048576 | tf_op jit(solution)/shard_map/all_to_all | solution.py:127
  18.4 28.8 %collective-permute-start = (bf16[2,2,2,131,128]{4,3,2,1,0:T(8,128)(2,1)S(1)}, bf16[2,2,2,131,128]{4,3,2,1,0:T(8,128)(2,1)S(1)}, u32[]{:S(2)}, u32[]{:S(2)}) collective-permute-start(bf16[2,2,2,131,128]{4,3,2,1,0:T(8,128)(2,1)S(1)} %get-tuple-element.21), channel_id=1, source_target_pairs={{0,2},{2,4},{4,6},{6,8},{8,10},{10,12},{12,14},{1,3},{3,5},{5,7},{... | collective-permute-start | bytes 804872 | tf_op jit(solution)/shard_map/ppermute | solution.py:23
  22.4 24.9 %collective-permute-start.1 = (bf16[2,2,2,131,128]{4,3,2,1,0:T(8,128)(2,1)S(1)}, bf16[2,2,2,131,128]{4,3,2,1,0:T(8,128)(2,1)S(1)}, u32[]{:S(2)}, u32[]{:S(2)}) collective-permute-start(bf16[2,2,2,131,128]{4,3,2,1,0:T(8,128)(2,1)S(1)} %get-tuple-element.22), channel_id=1, source_target_pairs={{2,0},{4,2},{6,4},{8,6},{10,8},{12,10},{14,12},{3,1},{5,3},{7,5},{... | collective-permute-start | bytes 804872 | tf_op jit(solution)/shard_map/ppermute | solution.py:25
  47.9 8.4 %slice-start.2 = ((s8[6291456]{0:T(1024)(128)(4,1)}), s8[2097152]{0:T(1024)(128)(4,1)S(1)}, s32[]{:S(2)}) async-start(s8[6291456]{0:T(1024)(128)(4,1)} %bitcast.314), calls=%async_computation.8 | async-start | bytes 4194304
  47.9 17.3 %all-to-all-start.2 = ((bf16[8,2,4,4096]{3,2,1,0:T(4,128)(2,1)}), bf16[8,2,4,4096]{3,2,1,0:T(4,128)(2,1)}, u32[]{:S(2)}, u32[]{:S(2)}) async-start(bf16[8,2,4,4096]{3,2,1,0:T(4,128)(2,1)} %copy.126), calls=%async_computation.2 | async-start | bytes 1048576 | tf_op jit(solution)/shard_map/all_to_all | solution.py:127
  52.2 4.1 %slice-start.3 = ((s8[6291456]{0:T(1024)(128)(4,1)}), s8[4194304]{0:T(1024)(128)(4,1)S(1)}, s32[]{:S(2)}) async-start(s8[6291456]{0:T(1024)(128)(4,1)} %bitcast.314), calls=%async_computation.9 | async-start | bytes 8388608
  65.2 8.0 %slice-start = ((s8[6291456]{0:T(1024)(128)(4,1)}), s8[2097152]{0:T(1024)(128)(4,1)S(1)}, s32[]{:S(2)}) async-start(s8[6291456]{0:T(1024)(128)(4,1)} %bitcast.297), calls=%async_computation.6 | async-start | bytes 4194304
  65.2 18.5 %all-to-all-start.4 = ((bf16[8,2,4,4096]{3,2,1,0:T(4,128)(2,1)}), bf16[8,2,4,4096]{3,2,1,0:T(4,128)(2,1)S(1)}, u32[]{:S(2)}, u32[]{:S(2)}) async-start(bf16[8,2,4,4096]{3,2,1,0:T(4,128)(2,1)} %copy.138), calls=%async_computation.4 | async-start | bytes 1048576 | tf_op jit(solution)/shard_map/all_to_all | solution.py:127
  69.0 4.3 %slice-start.1 = ((s8[6291456]{0:T(1024)(128)(4,1)}), s8[4194304]{0:T(1024)(128)(4,1)S(1)}, s32[]{:S(2)}) async-start(s8[6291456]{0:T(1024)(128)(4,1)} %bitcast.297), calls=%async_computation.7 | async-start | bytes 8388608
  83.7 15.2 %all-to-all-start.1 = ((bf16[8,2,4,2048]{3,1,2,0:T(2,128)(2,1)}), bf16[8,2,4,2048]{3,1,2,0:T(2,128)(2,1)S(1)}, u32[]{:S(2)}, u32[]{:S(2)}) async-start(bf16[8,2,4,2048]{3,1,2,0:T(2,128)(2,1)} %copy.118), calls=%async_computation.1 | async-start | bytes 524288 | tf_op jit(solution)/shard_map/all_to_all | solution.py:143
  99.0 14.5 %all-to-all-start.3 = ((bf16[8,2,4,2048]{3,1,2,0:T(2,128)(2,1)}), bf16[8,2,4,2048]{3,1,2,0:T(2,128)(2,1)S(1)}, u32[]{:S(2)}, u32[]{:S(2)}) async-start(bf16[8,2,4,2048]{3,1,2,0:T(2,128)(2,1)} %copy.130), calls=%async_computation.3 | async-start | bytes 524288 | tf_op jit(solution)/shard_map/all_to_all | solution.py:143
  106.5 15.0 %copy-start.7 = (f32[1,4,4096]{2,1,0:T(4,128)S(1)}, f32[1,4,4096]{2,1,0:T(4,128)}, u32[]{:S(2)}) copy-start(f32[1,4,4096]{2,1,0:T(4,128)} %get-tuple-element.25) | copy-start | bytes 196612
  106.5 15.3 %copy-start.6 = (f32[1,4,4096]{2,1,0:T(4,128)S(1)}, f32[1,4,4096]{2,1,0:T(4,128)}, u32[]{:S(2)}) copy-start(f32[1,4,4096]{2,1,0:T(4,128)} %get-tuple-element.26) | copy-start | bytes 196612
  106.5 22.2 %copy-start.5 = (f32[1,4,4096]{2,1,0:T(4,128)S(1)}, f32[1,4,4096]{2,1,0:T(4,128)}, u32[]{:S(2)}) copy-start(f32[1,4,4096]{2,1,0:T(4,128)} %get-tuple-element.27) | copy-start | bytes 196612
  113.4 15.2 %all-to-all-start.5 = ((bf16[8,2,4,2048]{3,1,2,0:T(2,128)(2,1)}), bf16[8,2,4,2048]{3,1,2,0:T(2,128)(2,1)S(1)}, u32[]{:S(2)}, u32[]{:S(2)}) async-start(bf16[8,2,4,2048]{3,1,2,0:T(2,128)(2,1)} %copy.142), calls=%async_computation.5 | async-start | bytes 524288 | tf_op jit(solution)/shard_map/all_to_all | solution.py:143
where the time goes:
time: 133 us; the launch traced here: 132 us
  starting transfers between devices  36 us (27%)
  matrix products  33.6 us (25%)
  blocking collectives  23.4 us (18%)
  waiting for transfers between devices  17.5 us (13%)
  local copies, waits for them, and re-layouts  14.7 us (11%)
  other arithmetic  4.67 us (4%)
  between operations  1.75 us (1%)
    all_to_all x3, starting transfers between devices, shards(): lax.all_to_all(answered, ('expert', 'group'), split_axis=0, concat_axis=0...  15.6 us
    all_to_all x3, starting transfers between devices, shards(): lax.all_to_all(flattened, ('expert', 'group'), split_axis=0, concat_axis=...  15.2 us
    unnamed x1, blocking collectives  13.5 us
    dot_general x3, matrix products, shards(): jnp.einsum('seki,eif->sekf', received, gate_weight, preferred_element_typ...  12.3 us
    all_to_all x3, waiting for transfers between devices, shards(): lax.all_to_all(answered, ('expert', 'group'), split_axis=0, concat_axis=0...  11.7 us
    dot_general x3, matrix products, shards(): jnp.einsum('seki,eif->sekf', received, up_weight, preferred_element_type=...  9.23 us
    dot_general x3, matrix products, shards(): jnp.einsum('sekf,efo->seko', hidden, down_weight, preferred_element_type=...  6.19 us
    all_gather x3, blocking collectives, shards(): hidden = lax.all_gather(hidden, 'tensor', axis=3, tiled=True)  5.97 us
  transfers between devices with their start and end apart: 8, of which 3 were waited for; matrix products, arithmetic and copies ran while one was open for 33% of the time, Pallas kernels for 0%

commit v1 on v0

--- a/solution.py
+++ b/solution.py
@@ -29,7 +29,7 @@
     return cells
 
 
-def shards(
+def grouped_shards(
     hidden_in,
     queries,
     new_keys,
@@ -172,7 +172,109 @@
     return (layer_out, resampled[0], resampled[1])
 
 
+def one_group_shards(
+    hidden_in,
+    queries,
+    new_keys,
+    new_values,
+    cache_keys,
+    cache_values,
+    route_ids,
+    route_weights,
+    norm_gain,
+    gate_weight,
+    up_weight,
+    down_weight,
+    ancestor_counts,
+):
+    step_count, token_count, query_heads, head_width = queries.shape
+    key_heads = cache_keys.shape[1]
+    cached = cache_keys.shape[2]
+    group_size = query_heads // key_heads
+    rows = step_count * token_count
+    model_width = hidden_in.shape[2]
+    expert_count = lax.axis_size("expert")
+    expert_index = lax.axis_index("expert")
+    expert_local = gate_weight.shape[0]
+    experts_all = expert_local * expert_count
+    column_width = down_weight.shape[2]
+    tensor_index = lax.axis_index("tensor")
+    cache_pair = jnp.stack([cache_keys, cache_values])
+    fresh_pair = jnp.transpose(jnp.stack([new_keys, new_values]), (0, 2, 3, 1, 4))
+    both_kv = jnp.concatenate([cache_pair, fresh_pair], axis=3)
+    length = both_kv.shape[3]
+    grouped = queries.reshape(step_count, token_count, key_heads, group_size, head_width)
+    scores = jnp.einsum(
+        "sphgd,phld->sphgl", grouped, both_kv[0], preferred_element_type=jnp.float32
+    ) / math.sqrt(head_width)
+    allowed = lax.broadcasted_iota(
+        jnp.int32, (step_count, length), 1
+    ) <= cached + lax.broadcasted_iota(jnp.int32, (step_count, length), 0)
+    scores = jnp.where(allowed[:, None, None, None, :], scores, -1e30)
+    exponent = jnp.exp(scores - jnp.max(scores, axis=-1, keepdims=True))
+    attn_weights = (exponent / jnp.sum(exponent, axis=-1, keepdims=True)).astype(jnp.bfloat16)
+    attended = jnp.einsum(
+        "sphgl,phld->sphgd", attn_weights, both_kv[1], preferred_element_type=jnp.float32
+    )
+    attended = attended.astype(jnp.bfloat16).reshape(rows, query_heads * head_width)
+    attended = lax.all_gather(attended, "tensor", axis=1, tiled=True)
+    residual = hidden_in.reshape(rows, model_width).astype(jnp.float32) + attended.astype(
+        jnp.float32
+    )
+    normed = (
+        residual
+        * lax.rsqrt(jnp.mean(residual * residual, axis=-1, keepdims=True) + epsilon)
+        * norm_gain
+    ).astype(jnp.bfloat16)
+    share = route_weights / jnp.sum(route_weights, axis=-1, keepdims=True)
+    hits = route_ids[..., None] == jnp.arange(experts_all, dtype=jnp.int32)
+    mix = jnp.sum(jnp.where(hits, share[..., None], 0.0), axis=2).reshape(rows, experts_all)
+    counts = jnp.broadcast_to(ancestor_counts.astype(jnp.float32)[None, :], (rows, token_count))
+    table = jnp.concatenate([mix, counts], axis=1)
+    spare = -table.shape[1] % 128
+    table = jnp.pad(table, ((0, 0), (0, spare)))
+    table = lax.all_gather(table, "expert", axis=0, tiled=True)
+    tokens = lax.all_gather(normed, "expert", axis=0, tiled=True)
+    gate = jnp.einsum("ri,eif->erf", tokens, gate_weight, preferred_element_type=jnp.float32)
+    up = jnp.einsum("ri,eif->erf", tokens, up_weight, preferred_element_type=jnp.float32)
+    gate = gate.astype(jnp.bfloat16).astype(jnp.float32)
+    up = up.astype(jnp.bfloat16).astype(jnp.float32)
+    hidden = (jax.nn.silu(gate) * up).astype(jnp.bfloat16)
+    hidden = lax.all_gather(hidden, "tensor", axis=2, tiled=True)
+    answered = jnp.einsum(
+        "erf,efo->ero", hidden, down_weight, preferred_element_type=jnp.float32
+    )
+    own_mix = lax.dynamic_slice_in_dim(table, expert_index * expert_local, expert_local, axis=1)
+    partial = jnp.sum(answered * own_mix.T[:, :, None], axis=0).astype(jnp.bfloat16)
+    returned = lax.all_to_all(
+        partial.reshape(expert_count, rows, column_width), "expert", 0, 0, tiled=True
+    )
+    expert_mix = jnp.sum(returned.astype(jnp.float32), axis=0)
+    own_columns = lax.dynamic_slice_in_dim(
+        residual, tensor_index * column_width, column_width, axis=1
+    )
+    half = (own_columns + expert_mix).astype(jnp.bfloat16)
+    layer_out = lax.all_gather(half, "tensor", axis=1, tiled=True).reshape(
+        step_count, token_count, model_width
+    )
+    every_count = table.reshape(expert_count, rows, -1)[
+        :, 0, experts_all : experts_all + token_count
+    ].reshape(-1)
+    running = jnp.cumsum(every_count.astype(jnp.int32))
+    first_index = expert_index * token_count
+    own_index = first_index + jnp.arange(token_count, dtype=jnp.int32)
+    ancestor = jnp.sum((running[None, :] <= own_index[:, None]).astype(jnp.int32), axis=1)
+    widened = padded(both_kv, ((("expert", "group"), 1),), REACH)
+    window_index = first_index - REACH + jnp.arange(token_count + 2 * REACH, dtype=jnp.int32)
+    selector = (ancestor[:, None] == window_index[None, :]).astype(jnp.bfloat16)
+    resampled = jnp.einsum(
+        "tw,kwhld->kthld", selector, widened, preferred_element_type=jnp.float32
+    ).astype(jnp.bfloat16)
+    return (layer_out, resampled[0], resampled[1])
+
+
 def solution(mesh):
+    shards = one_group_shards if mesh.shape["group"] == 1 else grouped_shards
     in_specs = (
         P(None, ("parts", "expert", "group"), None),
         P(None, ("parts", "expert", "group"), "tensor", None),

time: 133 us -> 118 us (0.89)
  blocking collectives: 23.4 us -> 77.2 us
  starting transfers between devices: 36 us -> 9.79 us
  matrix products: 33.6 us -> 7.53 us
  local copies, waits for them, and re-layouts: 14.7 us -> 7.75 us
  waiting for transfers between devices: 17.5 us -> 10.8 us
    all_gather x5, blocking collectives: 9.87 us -> 77.2 us  [the longest x1 36.5 us: one_group_shards(): table = lax.all_gather(table, 'expert', axis=0, tiled=True)]
    all_to_all x6 -> x1, starting transfers between devices: 30.8 us -> 3.49 us  [one_group_shards(): lax.all_to_all(partial.reshape(expert_count, rows, column_width), 'expert...]
    dot_general x24 -> x6, matrix products: 33.6 us -> 7.53 us  [the longest x1 4.06 us: one_group_shards(): jnp.einsum('ri,eif->erf', tokens, gate_weight, preferred_element_type=jnp...]
    unnamed x1 -> x0, blocking collectives: 13.5 us -> none
    all_to_all x6 -> x1, waiting for transfers between devices: 17.5 us -> 10.8 us  [one_group_shards(): lax.all_to_all(partial.reshape(expert_count, rows, column_width), 'expert...]
    reshape x7 -> x3, local copies, waits for them, and re-layouts: 4.06 us -> 0.75 us  [the longest x1 0.69 us: one_group_shards(): lax.all_gather(half, 'tensor', axis=1, tiled=True)]
    convert_element_type x10 -> x4, local copies, waits for them, and re-layouts: 3.49 us -> 0.97 us  [the longest x1 0.88 us: one_group_shards(): jnp.sum(answered * own_mix.T[:, :, None], axis=0).astype(jnp.bfloat16)]
    reduce_sum x6 -> x4, other arithmetic: 2.56 us -> 0.54 us  [the longest x1 0.18 us: one_group_shards(): jnp.sum((running[None, :] <= own_index[:, None]).astype(jnp.int32), axis=1)]
  transfers between devices with their start and end apart: 8 -> 3, of which waited for: 3 -> 1; matrix products, arithmetic and copies ran while one was open for 33% -> 13% of each run, Pallas kernels for 0% -> 0%
where the time goes in v1:
time: 118 us; the launch traced here: 117 us
  blocking collectives  77.2 us (65%)
  waiting for transfers between devices  10.8 us (9%)
  starting transfers between devices  9.79 us (8%)
  local copies, waits for them, and re-layouts  7.75 us (7%)
  matrix products  7.53 us (6%)
  other arithmetic  3.44 us (3%)
    all_gather x1, blocking collectives, one_group_shards(): table = lax.all_gather(table, 'expert', axis=0, tiled=True)  36.5 us
    all_gather x1, blocking collectives, one_group_shards(): tokens = lax.all_gather(normed, 'expert', axis=0, tiled=True)  34.9 us
    all_to_all x1, waiting for transfers between devices, one_group_shards(): lax.all_to_all(partial.reshape(expert_count, rows, column_width), 'expert...  10.8 us
    ppermute x1, starting transfers between devices, padded(): lax.ppermute(tail, axis, [(i, (i + 1) % count) for i in range(ends)])  5.01 us
    dot_general x1, matrix products, one_group_shards(): jnp.einsum('ri,eif->erf', tokens, gate_weight, preferred_element_type=jnp...  4.06 us
    all_to_all x1, starting transfers between devices, one_group_shards(): lax.all_to_all(partial.reshape(expert_count, rows, column_width), 'expert...  3.49 us
    unnamed x31, local copies, waits for them, and re-layouts  3.42 us
  transfers between devices with their start and end apart: 3, of which 1 were waited for; matrix products, arithmetic and copies ran while one was open for 13% of the time, Pallas kernels for 0%

profile of v1, /device:TPU:0, one launch (start us, length us, event | category | flops | bytes accessed | tf_op | source)
XLA Modules:
  0.0 117.5 jit_solution(2115568042403816963)
XLA Ops:
  0.7 0.8 copy_bitcast_fusion
  1.5 1.1 pad_maximum_fusion.1
  2.6 0.9 fusion.25
  3.4 5.0 %collective-permute-start = (bf16[2,2,2,131,128]{4,3,2,1,0:T(8,128)(2,1)}, bf16[2,2,2,131,128]{4,3,2,1,0:T(8,128)(2,1)S(1)}, u32[]{:S(2)}, u32[]{:S(2)}) collective-permute-start(bf16[2,2,2,131,128]{4,3,2,1,0:T(8,128)(2,1)} %get-tuple-element.17), channel_id=1, source_target_pairs={{0,2},{2,4},{4,6},{6,8},{8,10},{10,12},{12,14},{1,3},{3,5},{5,7},{... | collective-permute-start | bytes 804872 | tf_op jit(solution)/shard_map/ppermute | solution.py:23
  8.4 1.3 %collective-permute-start.1 = (bf16[2,2,2,131,128]{4,3,2,1,0:T(8,128)(2,1)}, bf16[2,2,2,131,128]{4,3,2,1,0:T(8,128)(2,1)}, u32[]{:S(2)}, u32[]{:S(2)}) collective-permute-start(bf16[2,2,2,131,128]{4,3,2,1,0:T(8,128)(2,1)} %get-tuple-element.18), channel_id=1, source_target_pairs={{2,0},{4,2},{6,4},{8,6},{10,8},{12,10},{14,12},{3,1},{5,3},{7,5},{... | collective-permute-start | bytes 804872 | tf_op jit(solution)/shard_map/ppermute | solution.py:25
  9.9 0.1 select_reduce_fusion
  10.2 36.5 %all-gather.1 = f32[8,12,128]{2,1,0:T(8,128)S(1)} all-gather(f32[1,12,128]{2,1,0:T(8,128)S(1)} %pad_bitcast_fusion), channel_id=1, replica_groups=mesh['parts'=2,'expert'=8,'group'=1,'tensor'=2] {'expert'}, dimensions={0}, use_global_device_ids=true | all-gather | bytes 55296 | tf_op jit(solution)/shard_map/all_gather | solution.py:236
  46.7 0.6 copy.46
  47.4 0.3 fusion.11
  47.6 0.2 fusion.26
  47.9 0.4 fusion.13
  48.3 1.9 %all_gather.15 = bf16[12,4096]{1,0:T(8,128)(2,1)S(1)} all-gather(bf16[12,2048]{1,0:T(8,128)(2,1)S(1)} %reshape.97), channel_id=1, replica_groups=mesh['parts'=2,'expert'=8,'group'=1,'tensor'=2] {'tensor'}, dimensions={1}, use_global_device_ids=true | all-gather | bytes 147456 | tf_op jit(solution)/shard_map/all_gather | solution.py:220
  50.2 0.2 multiply_reduce_fusion
  50.4 0.1 fusion.15
  50.5 34.9 %all-gather = bf16[8,12,4096]{2,1,0:T(8,128)(2,1)} all-gather(bf16[1,12,4096]{2,1,0:T(8,128)(2,1)S(1)} %fusion.15), channel_id=1, replica_groups=mesh['parts'=2,'expert'=8,'group'=1,'tensor'=2] {'expert'}, dimensions={0}, use_global_device_ids=true | all-gather | bytes 884736 | tf_op jit(solution)/shard_map/all_gather | solution.py:237
  85.4 1.5 %reshape.110 = bf16[96,4096,1]{1,0,2:T(8,128)(2,1)S(1)} reshape(bf16[8,12,4096]{2,1,0:T(8,128)(2,1)} %all-gather) | data formatting | bytes 1572864
  86.9 4.1 %fusion.9 = f32[2,96,384]{2,1,0:T(8,128)S(1)} fusion(bf16[96,4096,1]{1,0,2:T(8,128)(2,1)S(1)} %reshape.110, bf16[2,4096,384]{2,1,0:T(8,128)(2,1)} %param.22), kind=kOutput, calls=%fused_computation.13 | convolution fusion | flops 604127232 | bytes 7372800 | tf_op jit(solution)/shard_map/ri,eif->erf/dot_general | solution.py:238
  91.1 1.1 fusion.7
  92.2 2.0 %all_gather.17 = bf16[2,96,768]{2,1,0:T(8,128)(2,1)S(1)} all-gather(bf16[2,96,384]{2,1,0:T(8,128)(2,1)S(1)} %fusion.7), channel_id=1, replica_groups=mesh['parts'=2,'expert'=8,'group'=1,'tensor'=2] {'tensor'}, dimensions={2}, use_global_device_ids=true | all-gather | bytes 442368 | tf_op jit(solution)/shard_map/all_gather | solution.py:243
  94.2 1.2 fusion.1
  95.4 0.9 convert_element_type.103
  96.3 3.5 %all-to-all-start = ((bf16[8,12,2048]{2,1,0:T(8,128)(2,1)}), bf16[8,12,2048]{2,1,0:T(8,128)(2,1)S(1)}, u32[]{:S(2)}, u32[]{:S(2)}) async-start(bf16[8,12,2048]{2,1,0:T(8,128)(2,1)} %convert_element_type.103), calls=%async_computation | async-start | bytes 1048576 | tf_op jit(solution)/shard_map/all_to_all | solution.py:249
  100.0 0.1 reduce.1
  100.1 0.2 convert_reduce_fusion.1
  100.4 1.0 pad_maximum_fusion
  101.4 0.5 fusion.2
  101.9 0.2 slice_bitcast_fusion.4
  102.1 0.9 copy.50
  103.0 0.9 copy.49
  104.0 10.8 %all-to-all-done = bf16[8,12,2048]{2,1,0:T(8,128)(2,1)S(1)} async-done(((bf16[8,12,2048]{2,1,0:T(8,128)(2,1)}), bf16[8,12,2048]{2,1,0:T(8,128)(2,1)S(1)}, u32[]{:S(2)}, u32[]{:S(2)}) %all-to-all-start) | async-done | bytes 393248 | tf_op jit(solution)/shard_map/all_to_all | solution.py:249
  114.9 1.9 %all_gather.19 = bf16[12,4096]{1,0:T(8,128)(2,1)S(1)} all-gather(bf16[12,2048]{1,0:T(8,128)(2,1)S(1)} %add_convert_fusion), channel_id=1, replica_groups=mesh['parts'=2,'expert'=8,'group'=1,'tensor'=2] {'tensor'}, dimensions={1}, use_global_device_ids=true | all-gather | bytes 147456 | tf_op jit(solution)/shard_map/all_gather | solution.py:257
  116.8 0.7 reshape.99
  (52 shorter events, 0.9 us)
Async XLA Ops:
  0.6 46.7 %copy-start = (bf16[3,4,16,128]{3,2,1,0:T(8,128)(2,1)S(1)}, bf16[3,4,16,128]{3,2,1,0:T(8,128)(2,1)}, u32[]{:S(2)}) copy-start(bf16[3,4,16,128]{3,2,1,0:T(8,128)(2,1)} %param.14) | copy-start | bytes 147460
  0.6 9.1 %copy-start.8 = (s32[4]{0:T(128)S(1)}, s32[4]{0:T(128)}, u32[]{:S(2)}) copy-start(s32[4]{0:T(128)} %param.25) | copy-start | bytes 52
  0.7 9.2 %copy-start.7 = (f32[3,4,8]{2,1,0:T(4,128)S(1)}, f32[3,4,8]{2,1,0:T(4,128)}, u32[]{:S(2)}) copy-start(f32[3,4,8]{2,1,0:T(4,128)} %param.20) | copy-start | bytes 1156
  0.7 9.3 %copy-start.6 = (s32[3,4,8]{2,1,0:T(4,128)S(1)}, s32[3,4,8]{2,1,0:T(4,128)}, u32[]{:S(2)}) copy-start(s32[3,4,8]{2,1,0:T(4,128)} %param.19) | copy-start | bytes 1156
  0.7 46.7 %copy-start.3 = (bf16[3,4,4096]{2,1,0:T(4,128)(2,1)S(1)}, bf16[3,4,4096]{2,1,0:T(4,128)(2,1)}, u32[]{:S(2)}) copy-start(bf16[3,4,4096]{2,1,0:T(4,128)(2,1)} %param.13) | copy-start | bytes 294916
  3.4 47.0 %copy-start.4 = (f32[4096]{0:T(1024)S(1)}, f32[4096]{0:T(1024)}, u32[]{:S(2)}) copy-start(f32[4096]{0:T(1024)} %param.21) | copy-start | bytes 49156
  3.4 96.9 %collective-permute-start = (bf16[2,2,2,131,128]{4,3,2,1,0:T(8,128)(2,1)}, bf16[2,2,2,131,128]{4,3,2,1,0:T(8,128)(2,1)S(1)}, u32[]{:S(2)}, u32[]{:S(2)}) collective-permute-start(bf16[2,2,2,131,128]{4,3,2,1,0:T(8,128)(2,1)} %get-tuple-element.17), channel_id=1, source_target_pairs={{0,2},{2,4},{4,6},{6,8},{8,10},{10,12},{12,14},{1,3},{3,5},{5,7},{... | collective-permute-start | bytes 804872 | tf_op jit(solution)/shard_map/ppermute | solution.py:23
  8.4 91.9 %collective-permute-start.1 = (bf16[2,2,2,131,128]{4,3,2,1,0:T(8,128)(2,1)}, bf16[2,2,2,131,128]{4,3,2,1,0:T(8,128)(2,1)}, u32[]{:S(2)}, u32[]{:S(2)}) collective-permute-start(bf16[2,2,2,131,128]{4,3,2,1,0:T(8,128)(2,1)} %get-tuple-element.18), channel_id=1, source_target_pairs={{2,0},{4,2},{6,4},{8,6},{10,8},{12,10},{14,12},{3,1},{5,3},{7,5},{... | collective-permute-start | bytes 804872 | tf_op jit(solution)/shard_map/ppermute | solution.py:25
  85.4 5.6 %slice-start = ((s8[6291456]{0:T(1024)(128)(4,1)}), s8[2097152]{0:T(1024)(128)(4,1)S(1)}, s32[]{:S(2)}) async-start(s8[6291456]{0:T(1024)(128)(4,1)} %bitcast.66), calls=%async_computation.1 | async-start | bytes 4194304
  86.9 4.1 %slice-start.1 = ((s8[6291456]{0:T(1024)(128)(4,1)}), s8[4194304]{0:T(1024)(128)(4,1)S(1)}, s32[]{:S(2)}) async-start(s8[6291456]{0:T(1024)(128)(4,1)} %bitcast.66), calls=%async_computation.2 | async-start | bytes 8388608
  86.9 7.3 %slice-start.2 = ((s8[6291456]{0:T(1024)(128)(4,1)}), s8[4194304]{0:T(1024)(128)(4,1)S(1)}, s32[]{:S(2)}) async-start(s8[6291456]{0:T(1024)(128)(4,1)} %bitcast.68), calls=%async_computation.3 | async-start | bytes 8388608
  91.0 3.2 %slice-start.3 = ((s8[6291456]{0:T(1024)(128)(4,1)}), s8[2097152]{0:T(1024)(128)(4,1)S(1)}, s32[]{:S(2)}) async-start(s8[6291456]{0:T(1024)(128)(4,1)} %bitcast.68), calls=%async_computation.4 | async-start | bytes 4194304
  91.0 3.2 %copy-start.5 = (f32[2,96]{1,0:T(2,128)S(1)}, f32[2,96]{1,0:T(2,128)}, u32[]{:S(2)}) copy-start(f32[2,96]{1,0:T(2,128)} %copy.46) | copy-start | bytes 2308
  95.4 5.0 %copy-start.1 = (bf16[4,2,128,128]{3,2,1,0:T(8,128)(2,1)S(1)}, bf16[4,2,128,128]{3,2,1,0:T(8,128)(2,1)}, u32[]{:S(2)}) copy-start(bf16[4,2,128,128]{3,2,1,0:T(8,128)(2,1)} %param.18) | copy-start | bytes 786436
  95.4 5.0 %copy-start.2 = (bf16[4,2,128,128]{3,2,1,0:T(8,128)(2,1)S(1)}, bf16[4,2,128,128]{3,2,1,0:T(8,128)(2,1)}, u32[]{:S(2)}) copy-start(bf16[4,2,128,128]{3,2,1,0:T(8,128)(2,1)} %param.17) | copy-start | bytes 786436
  96.3 18.5 %all-to-all-start = ((bf16[8,12,2048]{2,1,0:T(8,128)(2,1)}), bf16[8,12,2048]{2,1,0:T(8,128)(2,1)S(1)}, u32[]{:S(2)}, u32[]{:S(2)}) async-start(bf16[8,12,2048]{2,1,0:T(8,128)(2,1)} %convert_element_type.103), calls=%async_computation | async-start | bytes 1048576 | tf_op jit(solution)/shard_map/all_to_all | solution.py:249

commit v2 on v0

--- a/solution.py
+++ b/solution.py
@@ -1,8 +1,11 @@
+import functools
 import math
 
 import jax
 import jax.numpy as jnp
 from jax import lax
+from jax.experimental import pallas as pl
+from jax.experimental.pallas import tpu as pltpu
 from jax.sharding import PartitionSpec as P
 
 REACH = 2
@@ -29,7 +32,7 @@
     return cells
 
 
-def shards(
+def grouped_shards(
     hidden_in,
     queries,
     new_keys,
@@ -172,7 +175,509 @@
     return (layer_out, resampled[0], resampled[1])
 
 
+MESH = pl.DeviceIdType.MESH
+CHUNKS = 2
+
+
+def step_kernel(
+    dims,
+    hidden_ref,
+    query_ref,
+    fresh_ref,
+    keys_ref,
+    values_ref,
+    table_ref,
+    gain_ref,
+    gate_hbm,
+    up_hbm,
+    down_hbm,
+    out_ref,
+    keys_out,
+    values_out,
+    both,
+    heads,
+    square,
+    tokens,
+    tables,
+    gate_w,
+    up_w,
+    down_w,
+    hidden,
+    parts,
+    returned,
+    halves,
+    halo,
+    weight_sem,
+    square_sem,
+    token_send,
+    token_recv,
+    pass_send,
+    pass_recv,
+    table_send,
+    table_recv,
+    hidden_sem,
+    part_send,
+    part_recv,
+    half_sem,
+    halo_sem,
+):
+    steps, toks, key_heads, cached, total, half = dims
+    rows = steps * toks
+    count = lax.axis_size("expert")
+    me = lax.axis_index("expert")
+    side = lax.axis_index("tensor")
+    other = 1 - side
+    peers = [lax.rem(me + k, count) for k in range(1, count)]
+    padded_rows = tokens.shape[2]
+    experts = gate_w.shape[0]
+    query_heads = query_ref.shape[2]
+    head_width = query_ref.shape[3]
+    bf16, f32 = jnp.bfloat16, jnp.float32
+
+    barrier = pltpu.get_barrier_semaphore()
+    for peer in peers:
+        pl.semaphore_signal(barrier, inc=1, device_id={"expert": peer}, device_id_type=MESH)
+    pl.semaphore_signal(barrier, inc=1, device_id={"tensor": other}, device_id_type=MESH)
+
+    loads = [
+        pltpu.make_async_copy(gate_hbm, gate_w, weight_sem.at[0]),
+        pltpu.make_async_copy(up_hbm, up_w, weight_sem.at[1]),
+        pltpu.make_async_copy(down_hbm, down_w, weight_sem.at[2]),
+    ]
+    for load in loads:
+        load.start()
+
+    tables[me] = table_ref[...]
+    both[0, :, :, 0:cached, :] = keys_ref[...]
+    both[1, :, :, 0:cached, :] = values_ref[...]
+    both[:, :, :, cached:, :] = fresh_ref[...]
+    length = both.shape[3]
+
+    step_rows = steps * query_heads
+    row = lax.broadcasted_iota(jnp.int32, (step_rows, length), 0)
+    lane = lax.broadcasted_iota(jnp.int32, (step_rows, length), 1)
+    allowed = lane <= cached + row // query_heads
+    head_of = (row % query_heads) // (query_heads // key_heads)
+    head_of_out = head_of[:, 0:head_width]
+    for p in range(toks):
+        q = jnp.concatenate([query_ref[s, p] for s in range(steps)], axis=0)
+        scores = jnp.zeros((step_rows, length), f32)
+        for h in range(key_heads):
+            one = lax.dot_general(
+                q, both[0, p, h], (((1,), (1,)), ((), ())), preferred_element_type=f32
+            )
+            scores = jnp.where(head_of == h, one, scores)
+        scores = jnp.where(allowed, scores / math.sqrt(head_width), -1e30)
+        exponent = jnp.exp(scores - jnp.max(scores, axis=-1, keepdims=True))
+        probs = (exponent / jnp.sum(exponent, axis=-1, keepdims=True)).astype(bf16)
+        mixed = jnp.zeros((step_rows, head_width), f32)
+        for h in range(key_heads):
+            one = jnp.dot(probs, both[1, p, h], preferred_element_type=f32)
+            mixed = jnp.where(head_of_out == h, one, mixed)
+        mixed = mixed.astype(bf16).astype(f32)
+        for s in range(steps):
+            at = (s * toks + p) * query_heads
+            heads[at : at + query_heads, :] = mixed[s * query_heads : (s + 1) * query_heads]
+    attended = jnp.concatenate(
+        [heads[pl.ds(h, rows, stride=query_heads), :] for h in range(query_heads)], axis=1
+    )
+    own_lanes = pl.ds(pl.multiple_of(side * half, half), half)
+    incoming = jnp.concatenate(
+        [hidden_ref[s, :, own_lanes].astype(f32) for s in range(steps)], axis=0
+    )
+    residual = incoming + attended
+    squares = jnp.sum(residual * residual, axis=-1, keepdims=True)
+    fill = jnp.zeros((padded_rows - rows, 128), f32)
+    square[0] = jnp.concatenate([jnp.broadcast_to(squares, (rows, 128)), fill], axis=0)
+
+    pl.semaphore_wait(barrier, count)
+
+    square_copy = pltpu.make_async_remote_copy(
+        src_ref=square.at[0],
+        dst_ref=square.at[1],
+        send_sem=square_sem.at[0],
+        recv_sem=square_sem.at[1],
+        device_id={"tensor": other},
+        device_id_type=MESH,
+    )
+    square_copy.start()
+
+    def table_copy(k):
+        return pltpu.make_async_remote_copy(
+            src_ref=tables.at[me],
+            dst_ref=tables.at[me],
+            send_sem=table_send.at[k],
+            recv_sem=table_recv.at[me],
+            device_id={"expert": peers[k]},
+            device_id_type=MESH,
+        )
+
+    for k in range(count - 1):
+        table_copy(k).start()
+
+    square_copy.wait()
+    mean = (square[0, 0:rows, 0:1] + square[1, 0:rows, 0:1]) / (2 * half)
+    normed = residual * lax.rsqrt(mean + epsilon) * gain_ref[:, own_lanes]
+    normed = jnp.concatenate([normed, jnp.zeros((padded_rows - rows, half), f32)], axis=0)
+    tokens[side, me] = normed.astype(bf16)
+
+    def token_copy(k):
+        return pltpu.make_async_remote_copy(
+            src_ref=tokens.at[side, me],
+            dst_ref=tokens.at[side, me],
+            send_sem=token_send.at[k],
+            recv_sem=token_recv.at[me],
+            device_id={"expert": peers[k]},
+            device_id_type=MESH,
+        )
+
+    def pass_copy(d):
+        return pltpu.make_async_remote_copy(
+            src_ref=tokens.at[side, d],
+            dst_ref=tokens.at[side, d],
+            send_sem=pass_send.at[d],
+            recv_sem=pass_recv.at[d],
+            device_id={"tensor": other},
+            device_id_type=MESH,
+        )
+
+    def arrival(buffer, sem, k):
+        d = peers[k]
+        return pltpu.make_async_remote_copy(
+            src_ref=buffer.at[d],
+            dst_ref=buffer.at[d],
+            send_sem=sem.at[d],
+            recv_sem=sem.at[d],
+            device_id={"expert": d},
+            device_id_type=MESH,
+        )
+
+    for k in range(count - 1):
+        token_copy(k).start()
+    pass_copy(me).start()
+    order = list(range(count - 1))
+    for k in order:
+        arrival(tokens.at[side], token_recv, k).wait_recv()
+        pass_copy(peers[k]).start()
+
+    def halo_copy(way):
+        first = toks - REACH if way == 0 else 0
+        return pltpu.make_async_remote_copy(
+            src_ref=both.at[:, first : first + REACH],
+            dst_ref=halo.at[way],
+            send_sem=halo_sem.at[0, way],
+            recv_sem=halo_sem.at[1, way],
+            device_id={"expert": lax.rem(me + (1 if way == 0 else count - 1), count)},
+            device_id_type=MESH,
+        )
+
+    @pl.when(me < count - 1)
+    def _():
+        halo_copy(0).start()
+
+    @pl.when(me > 0)
+    def _():
+        halo_copy(1).start()
+
+    loads[0].wait()
+    loads[1].wait()
+    all_rows = count * padded_rows
+    gates, ups = [], []
+    own_depth = pl.ds(pl.multiple_of(side * half, half), half)
+    other_depth = pl.ds(pl.multiple_of(other * half, half), half)
+    held = tokens[side].reshape(all_rows, half)
+    for e in range(experts):
+        gates.append(jnp.dot(held, gate_w[e, own_depth, :], preferred_element_type=f32))
+        ups.append(jnp.dot(held, up_w[e, own_depth, :], preferred_element_type=f32))
+
+    def pass_arrival(d):
+        return pltpu.make_async_remote_copy(
+            src_ref=tokens.at[other, d],
+            dst_ref=tokens.at[other, d],
+            send_sem=pass_send.at[d],
+            recv_sem=pass_recv.at[d],
+            device_id={"tensor": other},
+            device_id_type=MESH,
+        )
+
+    pass_arrival(me).wait_recv()
+    for k in order:
+        pass_arrival(peers[k]).wait_recv()
+    held = tokens[other].reshape(all_rows, half)
+
+    def hidden_copy(e):
+        return pltpu.make_async_remote_copy(
+            src_ref=hidden.at[side, e],
+            dst_ref=hidden.at[side, e],
+            send_sem=hidden_sem.at[0, e],
+            recv_sem=hidden_sem.at[1, e],
+            device_id={"tensor": other},
+            device_id_type=MESH,
+        )
+
+    def hidden_arrival(e):
+        return pltpu.make_async_remote_copy(
+            src_ref=hidden.at[other, e],
+            dst_ref=hidden.at[other, e],
+            send_sem=hidden_sem.at[0, e],
+            recv_sem=hidden_sem.at[1, e],
+            device_id={"tensor": other},
+            device_id_type=MESH,
+        )
+
+    for e in range(experts):
+        gate = gates[e] + jnp.dot(held, gate_w[e, other_depth, :], preferred_element_type=f32)
+        up = ups[e] + jnp.dot(held, up_w[e, other_depth, :], preferred_element_type=f32)
+        gate = gate.astype(bf16).astype(f32)
+        up = up.astype(bf16).astype(f32)
+        hidden[side, e] = (gate / (1.0 + jnp.exp(-gate)) * up).astype(bf16)
+        hidden_copy(e).start()
+
+    for k in order:
+        arrival(tables, table_recv, k).wait_recv()
+    everything = tables[...]
+    mix = everything[:, 0:padded_rows, :].reshape(all_rows, 128)
+    mix_lane = lax.broadcasted_iota(jnp.int32, (all_rows, 128), 1)
+    shares = [
+        jnp.sum(jnp.where(mix_lane == me * experts + e, mix, 0.0), axis=1, keepdims=True)
+        for e in range(experts)
+    ]
+
+    loads[2].wait()
+    activations = []
+    for e in range(experts):
+        hidden_arrival(e).wait_recv()
+        activations.append(jnp.concatenate([hidden[0, e], hidden[1, e]], axis=1))
+
+    def part_copy(c, k):
+        return pltpu.make_async_remote_copy(
+            src_ref=parts.at[c, peers[k]],
+            dst_ref=returned.at[c, me],
+            send_sem=part_send.at[c, k],
+            recv_sem=part_recv.at[c, me],
+            device_id={"expert": peers[k]},
+            device_id_type=MESH,
+        )
+
+    width = half // CHUNKS
+    for c in range(CHUNKS):
+        mixture = jnp.zeros((all_rows, width), f32)
+        for e in range(experts):
+            answered = jnp.dot(
+                activations[e],
+                down_w[e, :, c * width : (c + 1) * width],
+                preferred_element_type=f32,
+            )
+            mixture = mixture + shares[e] * answered
+        parts[c] = mixture.astype(bf16).reshape(count, padded_rows, width)
+        for k in order:
+            part_copy(c, k).start()
+
+    @pl.when(me > 0)
+    def _():
+        halo_copy(0).wait_recv()
+
+    @pl.when(me == 0)
+    def _():
+        halo[0] = jnp.zeros(halo.shape[1:], bf16)
+
+    @pl.when(me < count - 1)
+    def _():
+        halo_copy(1).wait_recv()
+
+    @pl.when(me == count - 1)
+    def _():
+        halo[1] = jnp.zeros(halo.shape[1:], bf16)
+
+    counts = jnp.sum(everything[:, padded_rows:, :], axis=0)
+    below = lax.broadcasted_iota(jnp.int32, (128, 128), 0)
+    above = lax.broadcasted_iota(jnp.int32, (128, 128), 1)
+    running = jnp.dot(
+        counts, jnp.where(below <= above, 1.0, 0.0).astype(f32), preferred_element_type=f32
+    )
+    running = jnp.broadcast_to(running[0:1], (8, 128))
+    place = me * toks + lax.broadcasted_iota(jnp.int32, (8, 128), 0)
+    which = lax.broadcasted_iota(jnp.int32, (8, 128), 1)
+    passed = jnp.where((running <= place.astype(f32)) & (which < total), 1.0, 0.0)
+    ancestor = jnp.sum(passed, axis=1, keepdims=True)
+    relative = ancestor - (me * toks - REACH).astype(f32)
+    for t in range(toks):
+        at = jnp.broadcast_to(relative[t : t + 1, :], (length, head_width))
+        picks = [
+            (w, jnp.where(at == float(w), 1.0, 0.0)) for w in range(t, t + 2 * REACH + 1)
+        ]
+        for kv, target in ((0, keys_out), (1, values_out)):
+            for h in range(key_heads):
+                chosen = jnp.zeros((length, head_width), f32)
+                for w, pick in picks:
+                    if w < REACH:
+                        source = halo[0, kv, w, h]
+                    elif w < REACH + toks:
+                        source = both[kv, w - REACH, h]
+                    else:
+                        source = halo[1, kv, w - REACH - toks, h]
+                    chosen = chosen + pick * source.astype(f32)
+                target[t, h] = chosen.astype(bf16)[0 : cached + steps]
+
+    sums = []
+    for c in range(CHUNKS):
+        for k in order:
+            arrival(returned.at[c], part_recv.at[c], k).wait_recv()
+        summed = parts[c, me].astype(f32)
+        for k in order:
+            summed = summed + returned[c, peers[k]].astype(f32)
+        sums.append(summed)
+    layer = residual + jnp.concatenate(sums, axis=1)[0:rows]
+    layer = jnp.concatenate([layer, jnp.zeros((padded_rows - rows, half), f32)], axis=0)
+    halves[side] = layer.astype(bf16)
+
+    def half_copy(which_half):
+        return pltpu.make_async_remote_copy(
+            src_ref=halves.at[which_half],
+            dst_ref=halves.at[which_half],
+            send_sem=half_sem.at[0],
+            recv_sem=half_sem.at[1],
+            device_id={"tensor": other},
+            device_id_type=MESH,
+        )
+
+    half_copy(side).start()
+    for k in order:
+        table_copy(k).wait_send()
+        token_copy(k).wait_send()
+        pass_copy(peers[k]).wait_send()
+        for c in range(CHUNKS):
+            part_copy(c, k).wait_send()
+    pass_copy(me).wait_send()
+    for e in range(experts):
+        hidden_copy(e).wait_send()
+
+    @pl.when(me < count - 1)
+    def _():
+        halo_copy(0).wait_send()
+
+    @pl.when(me > 0)
+    def _():
+        halo_copy(1).wait_send()
+
+    half_copy(other).wait_recv()
+    whole = jnp.concatenate([halves[0], halves[1]], axis=1).astype(f32)
+    for s in range(steps):
+        out_ref[s] = whole[s * toks : (s + 1) * toks].astype(bf16)
+    half_copy(side).wait_send()
+
+
+def one_group_shards(
+    hidden_in,
+    queries,
+    new_keys,
+    new_values,
+    cache_keys,
+    cache_values,
+    route_ids,
+    route_weights,
+    norm_gain,
+    gate_weight,
+    up_weight,
+    down_weight,
+    ancestor_counts,
+):
+    steps, toks, query_heads, head_width = queries.shape
+    key_heads, cached = cache_keys.shape[1:3]
+    rows = steps * toks
+    padded_rows = -(-rows // 16) * 16
+    length = -(-(cached + steps) // 16) * 16
+    model_width = hidden_in.shape[2]
+    half = down_weight.shape[2]
+    count = lax.axis_size("expert")
+    me = lax.axis_index("expert")
+    experts, _, units = gate_weight.shape
+    bf16, f32 = jnp.bfloat16, jnp.float32
+    fresh = jnp.transpose(jnp.stack([new_keys, new_values]), (0, 2, 3, 1, 4))
+    fresh = jnp.pad(fresh, ((0, 0), (0, 0), (0, 0), (0, length - cached - steps), (0, 0)))
+    share = route_weights / jnp.sum(route_weights, axis=-1, keepdims=True)
+    hits = route_ids[..., None] == jnp.arange(128, dtype=jnp.int32)
+    mix = jnp.sum(jnp.where(hits, share[..., None], 0.0), axis=2).reshape(rows, 128)
+    lanes = jnp.arange(128, dtype=jnp.int32)[None, :] - me * toks
+    counts = jnp.sum(
+        jnp.where(
+            lanes == jnp.arange(toks, dtype=jnp.int32)[:, None],
+            ancestor_counts.astype(f32)[:, None],
+            0.0,
+        ),
+        axis=0,
+        keepdims=True,
+    )
+    table = jnp.concatenate(
+        [
+            jnp.pad(mix, ((0, padded_rows - rows), (0, 0))),
+            jnp.pad(counts, ((0, 7), (0, 0))),
+        ],
+        axis=0,
+    )
+    dims = (steps, toks, key_heads, cached, count * toks, half)
+    vmem = pl.BlockSpec(memory_space=pltpu.VMEM)
+    hbm = pl.BlockSpec(memory_space=pl.ANY)
+    dma = pltpu.SemaphoreType.DMA
+    width = half // CHUNKS
+    return pl.pallas_call(
+        functools.partial(step_kernel, dims),
+        out_shape=(
+            jax.ShapeDtypeStruct(hidden_in.shape, bf16),
+            jax.ShapeDtypeStruct((toks, key_heads, cached + steps, head_width), bf16),
+            jax.ShapeDtypeStruct((toks, key_heads, cached + steps, head_width), bf16),
+        ),
+        in_specs=[vmem] * 7 + [hbm] * 3,
+        out_specs=(vmem, vmem, vmem),
+        scratch_shapes=[
+            pltpu.VMEM((2, toks, key_heads, length, head_width), bf16),
+            pltpu.VMEM((rows * query_heads, head_width), f32),
+            pltpu.VMEM((2, padded_rows, 128), f32),
+            pltpu.VMEM((2, count, padded_rows, half), bf16),
+            pltpu.VMEM((count, padded_rows + 8, 128), f32),
+            pltpu.VMEM(gate_weight.shape, bf16),
+            pltpu.VMEM(up_weight.shape, bf16),
+            pltpu.VMEM(down_weight.shape, bf16),
+            pltpu.VMEM((2, experts, count * padded_rows, units), bf16),
+            pltpu.VMEM((CHUNKS, count, padded_rows, width), bf16),
+            pltpu.VMEM((CHUNKS, count, padded_rows, width), bf16),
+            pltpu.VMEM((2, padded_rows, half), bf16),
+            pltpu.VMEM((2, 2, REACH, key_heads, length, head_width), bf16),
+            dma((3,)),
+            dma((2,)),
+            dma((count,)),
+            dma((count,)),
+            dma((count,)),
+            dma((count,)),
+            dma((count,)),
+            dma((count,)),
+            dma((2, experts)),
+            dma((CHUNKS, count)),
+            dma((CHUNKS, count)),
+            dma((2,)),
+            dma((2, 2)),
+        ],
+        compiler_params=pltpu.CompilerParams(
+            collective_id=0, has_side_effects=True, vmem_limit_bytes=48 * 2**20
+        ),
+        name="step_kernel",
+    )(
+        hidden_in,
+        queries,
+        fresh,
+        cache_keys,
+        cache_values,
+        table,
+        norm_gain[None, :],
+        gate_weight,
+        up_weight,
+        down_weight,
+    )
+
+
 def solution(mesh):
+    fits = mesh.shape["group"] == 1 and mesh.shape["tensor"] == 2
+    shards = one_group_shards if fits else grouped_shards
     in_specs = (
         P(None, ("parts", "expert", "group"), None),
         P(None, ("parts", "expert", "group"), "tensor", None),

time: 133 us -> 50.4 us (0.38)
  the two profiles are of different devices: /device:TPU:0 before, /device:TPU:25 now
where the time goes in v2:
time: 50.4 us; the launch traced here: 49.9 us
  Pallas kernels  39.3 us (78%)
  local copies, waits for them, and re-layouts  7.51 us (15%)
  other arithmetic  2.42 us (5%)
  between operations  0.69 us (1%)
    pallas_call x1, Pallas kernels, one_group_shards(): pl.pallas_call(functools.partial(step_kernel, dims), out_shape=(jax.Shape...  39.3 us
    unnamed x11, local copies, waits for them, and re-layouts  4.94 us
    pallas_call x2, local copies, waits for them, and re-layouts, one_group_shards(): pl.pallas_call(functools.partial(step_kernel, dims), out_shape=(jax.Shape...  1.82 us

profile of v2, /device:TPU:25, one launch (start us, length us, event | category | flops | bytes accessed | tf_op | source)
XLA Modules:
  0.0 49.9 jit_solution(14741368155602452270)
XLA Ops:
  0.6 0.7 %convert_element_type.9 = f32[4]{0:T(128)S(1)} convert(s32[4]{0:T(128)} %param.25) | non-fusion elementwise | flops 4 | bytes 32 | tf_op jit(solution)/shard_map/convert_element_type | solution.py:605
  1.3 0.1 select_reduce_fusion.1
  1.4 0.8 %fusion.1 = f32[3,4,8]{2,1,0:T(4,128)S(1)} fusion(f32[3,4,8]{2,1,0:T(4,128)} %param.20), kind=kOutput, calls=%fused_computation.9 | output fusion | flops 115 | bytes 768 | tf_op jit(solution)/shard_map/div | solution.py:598
  2.2 0.8 %select_reduce_fusion = f32[3,4,128]{2,1,0:T(4,128)S(1)} fusion(f32[3,4,8]{2,1,0:T(4,128)S(1)} %fusion.1, s32[3,4,8]{2,1,0:T(4,128)} %param.19), kind=kLoop, calls=%fused_computation | loop fusion | flops 35328 | bytes 6912 | tf_op jit(solution)/shard_map/reduce_sum | solution.py:600
  3.1 0.7 %copy_bitcast_fusion = (bf16[1,3,4,2,128]{4,1,3,2,0:T(4,128)(2,1)S(1)}, bf16[1,3,4,2,128]{4,1,3,2,0:T(4,128)(2,1)S(1)}) fusion(bf16[3,4,2,128]{3,2,1,0:T(2,128)(2,1)} %param.16, bf16[3,4,2,128]{3,2,1,0:T(2,128)(2,1)} %param.15), kind=kLoop, calls=%fused_computation.6 | loop fusion | bytes 24576 | tf_op jit(solution)/shard_map/stack | solution.py:596
  3.8 0.0 copy-start
  3.8 0.9 %copy-done = bf16[4,2,128,128]{3,2,1,0:T(8,128)(2,1)S(1)} copy-done((bf16[4,2,128,128]{3,2,1,0:T(8,128)(2,1)S(1)}, bf16[4,2,128,128]{3,2,1,0:T(8,128)(2,1)}, u32[]{:S(2)}) %copy-start) | copy-done | bytes 262168
  4.8 0.0 copy-start.1
  4.8 0.9 %copy-done.1 = bf16[4,2,128,128]{3,2,1,0:T(8,128)(2,1)S(1)} copy-done((bf16[4,2,128,128]{3,2,1,0:T(8,128)(2,1)S(1)}, bf16[4,2,128,128]{3,2,1,0:T(8,128)(2,1)}, u32[]{:S(2)}) %copy-start.1) | copy-done | bytes 262168
  5.7 0.0 copy-start.2
  5.7 0.9 %copy-done.2 = bf16[3,4,4096]{2,1,0:T(4,128)(2,1)S(1)} copy-done((bf16[3,4,4096]{2,1,0:T(4,128)(2,1)S(1)}, bf16[3,4,4096]{2,1,0:T(4,128)(2,1)}, u32[]{:S(2)}) %copy-start.2) | copy-done | bytes 98328
  6.6 0.0 copy-start.3
  6.6 0.8 %copy-done.3 = bf16[3,4,16,128]{3,2,1,0:T(8,128)(2,1)S(1)} copy-done((bf16[3,4,16,128]{3,2,1,0:T(8,128)(2,1)S(1)}, bf16[3,4,16,128]{3,2,1,0:T(8,128)(2,1)}, u32[]{:S(2)}) %copy-start.3) | copy-done | bytes 49176
  7.4 0.0 copy-start.4
  7.4 0.7 %copy-done.4 = f32[4096]{0:T(1024)S(1)} copy-done((f32[4096]{0:T(1024)S(1)}, f32[4096]{0:T(1024)}, u32[]{:S(2)}) %copy-start.4) | copy-done | bytes 16408
  8.1 39.3 %step_kernel.1 = (bf16[3,4,4096]{2,1,0:T(4,128)(2,1)S(1)}, bf16[4,2,131,128]{3,2,1,0:T(8,128)(2,1)S(1)}, bf16[4,2,131,128]{3,2,1,0:T(8,128)(2,1)S(1)}) custom-call(bf16[3,4,4096]{2,1,0:T(4,128)(2,1)S(1)} %copy-done.2, bf16[3,4,16,128]{3,2,1,0:T(8,128)(2,1)S(1)} %copy-done.3, bf16[2,4,2,16,128]{4,3,2,1,0:T(8,128)(2,1)S(1)} %pad.12.fresh_ref, ...), custom_call_target="tpu_custom_call" | custom-call | tf_op jit(solution)/shard_map/step_kernel/pallas_call | solution.py:623
  47.4 0.9 %copy.22 = bf16[4,2,131,128]{3,1,2,0:T(2,128)(2,1)} copy(bf16[4,2,131,128]{3,2,1,0:T(8,128)(2,1)S(1)} %get-tuple-element.7) | data formatting | bytes 536576 | tf_op jit(solution)/shard_map/step_kernel/pallas_call | solution.py:623
  48.4 0.9 %copy.23 = bf16[4,2,131,128]{3,1,2,0:T(2,128)(2,1)} copy(bf16[4,2,131,128]{3,2,1,0:T(8,128)(2,1)S(1)} %get-tuple-element.8) | data formatting | bytes 536576 | tf_op jit(solution)/shard_map/step_kernel/pallas_call | solution.py:623
  49.3 0.6 %copy.27 = bf16[3,4,4096]{2,1,0:T(4,128)(2,1)} copy(bf16[3,4,4096]{2,1,0:T(4,128)(2,1)S(1)} %get-tuple-element.14) | data formatting | bytes 196608
  (5 shorter events, 0.0 us)
Async XLA Ops:
  3.8 1.0 %copy-start = (bf16[4,2,128,128]{3,2,1,0:T(8,128)(2,1)S(1)}, bf16[4,2,128,128]{3,2,1,0:T(8,128)(2,1)}, u32[]{:S(2)}) copy-start(bf16[4,2,128,128]{3,2,1,0:T(8,128)(2,1)} %keys_ref.1) | copy-start | bytes 786436
  4.8 0.9 %copy-start.1 = (bf16[4,2,128,128]{3,2,1,0:T(8,128)(2,1)S(1)}, bf16[4,2,128,128]{3,2,1,0:T(8,128)(2,1)}, u32[]{:S(2)}) copy-start(bf16[4,2,128,128]{3,2,1,0:T(8,128)(2,1)} %values_ref.1) | copy-start | bytes 786436
  5.7 0.9 %copy-start.2 = (bf16[3,4,4096]{2,1,0:T(4,128)(2,1)S(1)}, bf16[3,4,4096]{2,1,0:T(4,128)(2,1)}, u32[]{:S(2)}) copy-start(bf16[3,4,4096]{2,1,0:T(4,128)(2,1)} %hidden_ref.1) | copy-start | bytes 294916
  6.6 0.8 %copy-start.3 = (bf16[3,4,16,128]{3,2,1,0:T(8,128)(2,1)S(1)}, bf16[3,4,16,128]{3,2,1,0:T(8,128)(2,1)}, u32[]{:S(2)}) copy-start(bf16[3,4,16,128]{3,2,1,0:T(8,128)(2,1)} %query_ref.1) | copy-start | bytes 147460
  7.4 0.7 %copy-start.4 = (f32[4096]{0:T(1024)S(1)}, f32[4096]{0:T(1024)}, u32[]{:S(2)}) copy-start(f32[4096]{0:T(1024)} %param.21) | copy-start | bytes 49156
